TPU v7x, 256 devices: a whole 4x4x8 slice. The times are simulated.
256 devices in a mesh: blk: 64 (over x_hi, z, y), tp: 4 (over x_lo, core).
Axes of the slice: x: 4 (x_hi: 2, x_lo: 2; x = x_hi * 2 + x_lo), y: 4, z: 8, core: 2. Of those that a mesh axis runs over, the one named last changes fastest.
Arguments:
- text_query: bfloat16 [8192, 4096], P('blk', 'tp'), may hold values from -4.5 to 4.5
- text_keyval: bfloat16 [2, 8192, 4096], P(None, 'blk', 'tp'), may hold values from -4.5 to 4.5
- frame_features: bfloat16 [16384, 1024], P(('blk', 'tp')), may hold values from -6 to 6
- frame_proj: bfloat16 [1024, 3, 4096], P(None, None, 'tp'), may hold values from -0.1875 to 0.1875
- frame_slot: int32 [64, 4], P('blk'), may hold values from 0 to 3, each once within a row
- counts: int32 [64, 2], replicated, may hold values from 0 to 128, as said below
- block_mask: int32 [64, 4], P('blk'), may hold values from 0 to 1, as said below
Outputs:
- attended: bfloat16 [24576, 4096], P('blk', 'tp')
Inputs may be any that keep to these rules, and one draw needn't show every extreme that they name: `frame_slot`: each row is an ordering of the block's 4 encoded frames. `counts`: row b holds block b's live frames (0 to 4) and live text tokens (2 to 128); in every draw some block has 4 live frames, some has none, and some has 128 live text tokens. `block_mask`: column 0 is all ones; entry [c, d] is 0 where d > c; some row is all ones.
All inputs are finite; a program needn't handle non-finite values.
Results may differ from a plain program's by a relative error of at most 0.0065.
Values may be sent and summed in bfloat16 or wider, within the bound.
No kernel may reach another device: no remote copies, remote signals or barrier semaphores. Data moves between devices by JAX's collectives and lax.ppermute only.
A program may use at most 64 MiB of HBM per device.

v0:
```python
import math

import jax
import jax.numpy as jnp
from jax import lax
from jax.sharding import PartitionSpec as P

HD = 128
FT = 64
REACH = 4


def from_behind(value, axis, by):
    length = lax.axis_size(axis)
    pairs = [(i, i + by) for i in range(length) if 0 <= i + by < length]
    return lax.ppermute(value, axis, pairs)


def live_slots(count_row, frame_rows, text_cap):
    slots = jnp.arange(frame_rows + text_cap, dtype=jnp.int32)
    frame_live = (slots < frame_rows) & (slots // FT < count_row[0])
    text_live = (slots >= frame_rows) & (slots - frame_rows < count_row[1])
    return frame_live | text_live


def block_partial(queries, pair, allowed):
    heads = queries.shape[1]
    span = pair.shape[1]
    keys = pair[0].reshape(span, heads, HD)
    values = pair[1].reshape(span, heads, HD)
    scores = jnp.einsum("qhd,khd->hqk", queries, keys, preferred_element_type=jnp.float32) * (
        1.0 / math.sqrt(HD)
    )
    scores = jnp.where(allowed[None], scores, -1e30)
    row_max = jnp.max(scores, axis=2)
    expo = jnp.exp(scores - row_max[:, :, None])
    normalizer = jnp.sum(expo, axis=2)
    weights = expo.astype(jnp.bfloat16)
    weighted = jnp.einsum("hqk,khd->hqd", weights, values, preferred_element_type=jnp.float32)
    return (row_max, weighted, normalizer)


def absorb(running, incoming):
    old_max, old_weighted, old_norm = running
    new_max, new_weighted, new_norm = incoming
    joint = jnp.maximum(old_max, new_max)
    keep_old = jnp.exp(old_max - joint)
    keep_new = jnp.exp(new_max - joint)
    weighted = old_weighted * keep_old[:, :, None] + new_weighted * keep_new[:, :, None]
    return (joint, weighted, old_norm * keep_old + new_norm * keep_new)


def norm_project(rows, weights):
    feats = rows.astype(jnp.float32)
    normed = feats * lax.rsqrt(jnp.mean(feats * feats, axis=1, keepdims=True) + 1e-05)
    return jnp.einsum(
        "rv,vmc->rmc", normed.astype(jnp.bfloat16), weights, preferred_element_type=jnp.float32
    ).astype(jnp.bfloat16)


def body(text_query, text_keyval, frame_features, frame_proj, frame_slot, counts, block_mask):
    width = text_query.shape[1]
    heads = width // HD
    text_cap = text_query.shape[0]
    frame_cap = frame_slot.shape[1]
    frame_rows = frame_cap * FT
    span = frame_rows + text_cap
    block_index = lax.axis_index("blk")
    projected = norm_project(lax.all_gather(frame_features, "tp", axis=0, tiled=True), frame_proj)
    placed = jnp.take(projected.reshape(frame_cap, FT, 3, width), frame_slot[0], axis=0).reshape(
        frame_rows, 3, width
    )
    queries = jnp.concatenate([placed[:, 0], text_query], axis=0).reshape(span, heads, HD)
    key_rows = jnp.concatenate([placed[:, 1], text_keyval[0]], axis=0)
    value_rows = jnp.concatenate([placed[:, 2], text_keyval[1]], axis=0)
    own_pair = jnp.stack([key_rows, value_rows])
    slots = jnp.arange(span, dtype=jnp.int32)
    query_live = live_slots(counts[block_index], frame_rows, text_cap)
    running = block_partial(
        queries, own_pair, query_live[None, :] & (slots[:, None] >= slots[None, :])
    )
    arrived = own_pair
    for distance in range(1, REACH):
        arrived = from_behind(arrived, "blk", 1)
        source = jnp.maximum(block_index - distance, 0)
        key_live = live_slots(counts[source], frame_rows, text_cap)

        def include(carried):
            allowed = jnp.broadcast_to(key_live[None, :], (span, span))
            return absorb(carried, block_partial(queries, arrived, allowed))

        def exclude(carried):
            return carried

        running = lax.cond(block_mask[0, distance] > 0, include, exclude, running)
    row_max, weighted, normalizer = running
    result = weighted / normalizer[:, :, None]
    result = jnp.transpose(result, (1, 0, 2)).reshape(span, width)
    result = jnp.where(query_live[:, None], result, 0.0)
    return result.astype(jnp.bfloat16)


def solution(mesh):
    placed = (
        P("blk", "tp"),
        P(None, "blk", "tp"),
        P(("blk", "tp"), None),
        P(None, None, "tp"),
        P("blk", None),
        P(),
        P("blk", None),
    )
    return jax.shard_map(
        body, mesh=mesh, in_specs=placed, out_specs=P("blk", "tp"), check_vma=False
    )
```

profile of v0, /device:TPU:6, one launch (start us, length us, event | category | flops | bytes accessed | tf_op | source)
XLA Modules:
  0.0 165.5 jit_solution(15687413513281191632)
XLA Ops:
  1.3 2.0 %slice_bitcast_fusion.1 = (bf16[128,1024]{1,0:T(8,128)(2,1)S(1)}, bf16[128,1024]{1,0:T(8,128)(2,1)}, bf16[1,128,1024]{2,1,0:T(8,128)(2,1)}, bf16[1,128,1024]{2,1,0:T(8,128)(2,1)}) fusion(bf16[2,128,1024]{2,1,0:T(8,128)(2,1)} %param.14), kind=kLoop, calls=%fused_computation.114 | loop fusion | bytes 1572864 | tf_op jit(solution)/shard_map/squeeze | solution.py:74
  3.3 7.0 %all_gather.3 = bf16[256,1024]{1,0:T(8,128)(2,1)S(1)} all-gather(bf16[64,1024]{1,0:T(8,128)(2,1)} %param.15), channel_id=1, replica_groups=mesh['blk'=64,'tp'=4] {'tp'}, dimensions={0}, use_global_device_ids=true | all-gather | bytes 655360 | tf_op jit(solution)/shard_map/all_gather | solution.py:69
  10.5 4.7 %convolution_convert_fusion = bf16[256,3,1024]{2,0,1:T(8,128)(2,1)S(1)} fusion(bf16[1024,3,1024]{2,0,1:T(8,128)(2,1)} %param.16, bf16[256,1024]{1,0:T(8,128)(2,1)S(1)} %all_gather.3, f32[256]{0:T(256)S(1)} %add_rsqrt_fusion), kind=kOutput, calls=%fused_computation.65 | convolution fusion | flops 1612185600 | bytes 8389632 | tf_op jit(solution)/shard_map/rv,vmc->rmc/dot_general | solution.py:56
  17.8 3.6 %collective-permute-start = (bf16[2,384,1024]{2,1,0:T(8,128)(2,1)S(1)}, bf16[2,384,1024]{2,1,0:T(8,128)(2,1)}, u32[]{:S(2)}, u32[]{:S(2)}) collective-permute-start(bf16[2,384,1024]{2,1,0:T(8,128)(2,1)S(1)} %pad_maximum_fusion), channel_id=1, source_target_pairs={{0,4},{4,8},{8,12},{12,16},{16,20},{20,24},{24,28},{28,32},{32,36}... | collective-permute-start | bytes 4718600 | tf_op jit(solution)/shard_map/ppermute | solution.py:16
  21.4 42.6 %collective-permute-done = bf16[2,384,1024]{2,1,0:T(8,128)(2,1)} collective-permute-done((bf16[2,384,1024]{2,1,0:T(8,128)(2,1)S(1)}, bf16[2,384,1024]{2,1,0:T(8,128)(2,1)}, u32[]{:S(2)}, u32[]{:S(2)}) %collective-permute-start) | collective-permute-done | bytes 1572896 | tf_op jit(solution)/shard_map/ppermute | solution.py:16
  64.0 1.9 %collective-permute-start.1 = (bf16[2,384,1024]{2,1,0:T(8,128)(2,1)}, bf16[2,384,1024]{2,1,0:T(8,128)(2,1)}, u32[]{:S(2)}, u32[]{:S(2)}) collective-permute-start(bf16[2,384,1024]{2,1,0:T(8,128)(2,1)} %collective-permute-done), channel_id=1, source_target_pairs={{0,4},{4,8},{8,12},{12,16},{16,20},{20,24},{24,28},{28,32},{32,36}... | collective-permute-start | bytes 4718600 | tf_op jit(solution)/shard_map/ppermute | solution.py:16
  71.7 1.2 and_or_fusion.3
  73.1 34.9 %collective-permute-done.1 = bf16[2,384,1024]{2,1,0:T(8,128)(2,1)} collective-permute-done((bf16[2,384,1024]{2,1,0:T(8,128)(2,1)}, bf16[2,384,1024]{2,1,0:T(8,128)(2,1)}, u32[]{:S(2)}, u32[]{:S(2)}) %collective-permute-start.1) | collective-permute-done | bytes 1572896 | tf_op jit(solution)/shard_map/ppermute | solution.py:16
  108.0 1.9 %collective-permute-start.2 = (bf16[2,384,1024]{2,1,0:T(8,128)(2,1)}, bf16[2,384,1024]{2,1,0:T(8,128)(2,1)}, u32[]{:S(2)}, u32[]{:S(2)}) collective-permute-start(bf16[2,384,1024]{2,1,0:T(8,128)(2,1)} %collective-permute-done.1), channel_id=1, source_target_pairs={{0,4},{4,8},{8,12},{12,16},{16,20},{20,24},{24,28},{28,32},{32,36}... | collective-permute-start | bytes 4718600 | tf_op jit(solution)/shard_map/ppermute | solution.py:16
  110.9 1.0 fusion.42
  111.8 2.6 %fusion.44 = f32[8,384,128]{2,1,0:T(8,128)} fusion(f32[8,384,384]{1,2,0:T(8,128)S(1)} %get-tuple-element.309, f32[8,384]{1,0:T(8,128)S(1)} %get-tuple-element.308, pred[384,384]{0,1:T(8,128)(4,1)S(1)} %fusion.60, bf16[128,8,128]{2,0,1:T(8,128)(2,1)S(1)} %copy.83, bf16[256,8,128]{2,0,1:T(8,128)(2,1)S(1)} %copy.82), kind=kOutput, calls=%fused_computation.60 | convolution fusion | flops 308281344 | bytes 7237632 | tf_op jit(solution)/shard_map/hqk,khd->hqd/dot_general | solution.py:39
  114.5 1.3 and_or_fusion.2
  115.9 9.0 %conditional.3 = ((f32[8,384]{1,0:T(8,128)S(1)}, f32[8,384,128]{2,1,0:T(8,128)}, f32[8,384]{1,0:T(8,128)S(1)})) conditional(s32[]{:T(128)} %bitcast.14, (f32[8,384]{1,0:T(8,128)S(1)}, f32[8,384,128]{2,1,0:T(8,128)}, f32[8,384]{1,0:T(8,128)S(1)}) %tuple.31, (pred[384]{0:T(512)(128)(4,1)S(1)}, bf16[2,384,1024]{2,1,0:T(8,128)(2,1)}, ...), branch_computations={%region_3.4_spmd, %region_4.7_spmd} | conditional | flops 618147840 | bytes 26125472 | solution.py:95
  116.1 1.9 %copy.85 = bf16[2,384,1024]{1,2,0:T(8,128)(2,1)S(1)} copy(bf16[2,384,1024]{2,1,0:T(8,128)(2,1)} %get-tuple-element.236) | data formatting | bytes 3145728 | tf_op jit(solution)/shard_map
  118.1 1.4 fusion
  119.5 1.1 fusion.1
  120.6 4.3 %multiply_add_fusion = f32[8,384,128]{2,1,0:T(8,128)} fusion(f32[8,384,128]{2,1,0:T(8,128)} %get-tuple-element.167, bf16[384,8,128]{0,2,1:T(8,128)(2,1)S(1)} %bitcast.77, f32[8,384,384]{1,2,0:T(8,128)S(1)} %get-tuple-element.277, f32[8,384]{1,0:T(8,128)S(1)} %get-tuple-element.276, pred[384]{0:T(512)(128)(4,1)S(1)} %get-tuple-element.164, ...), kind=kOutput, calls=%fused_computation.11 | convolution fusion | flops 307888128 | bytes 8688000 | tf_op jit(solution)/shard_map/cond/branch_1_fun/hqk,khd->hqd/dot_general | solution.py:39
  124.9 10.8 %conditional.4 = ((f32[8,384]{1,0:T(8,128)S(1)}, f32[8,384,128]{2,1,0:T(8,128)}, f32[8,384]{1,0:T(8,128)S(1)})) conditional(s32[]{:T(128)} %bitcast.13, (f32[8,384]{1,0:T(8,128)S(1)}, f32[8,384,128]{2,1,0:T(8,128)}, f32[8,384]{1,0:T(8,128)S(1)}) %get-tuple-element.334, (s32[]{:T(128)}, s32[64,2]{0,1:T(2,128)S(1)}, s32[384]{0:T(512)S(1)}, ...), branch_computations={%region_7.8_spmd, %region_8.11_spmd} | conditional | flops 618149760 | bytes 26129764 | solution.py:95
  125.5 1.3 and_or_fusion
  126.8 1.9 %copy.86 = bf16[2,384,1024]{1,2,0:T(8,128)(2,1)S(1)} copy(bf16[2,384,1024]{2,1,0:T(8,128)(2,1)} %get-tuple-element.247) | data formatting | bytes 3145728 | tf_op jit(solution)/shard_map
  128.9 1.4 fusion.13
  130.2 1.1 fusion.14
  131.4 4.3 %multiply_add_fusion.2 = f32[8,384,128]{2,1,0:T(8,128)} fusion(f32[8,384,128]{2,1,0:T(8,128)} %get-tuple-element.178, bf16[384,8,128]{0,2,1:T(8,128)(2,1)S(1)} %bitcast.76, f32[8,384,384]{1,2,0:T(8,128)S(1)} %get-tuple-element.283, f32[8,384]{1,0:T(8,128)S(1)} %get-tuple-element.282, pred[384]{0:T(512)(128)(4,1)S(1)} %and_or_fusion, ...), kind=kOutput, calls=%fused_computation.27 | convolution fusion | flops 307888128 | bytes 8688000 | tf_op jit(solution)/shard_map/cond/branch_1_fun/hqk,khd->hqd/dot_general | solution.py:39
  135.7 15.5 %collective-permute-done.2 = bf16[2,384,1024]{2,1,0:T(8,128)(2,1)} collective-permute-done((bf16[2,384,1024]{2,1,0:T(8,128)(2,1)}, bf16[2,384,1024]{2,1,0:T(8,128)(2,1)}, u32[]{:S(2)}, u32[]{:S(2)}) %collective-permute-start.2) | collective-permute-done | bytes 1572896 | tf_op jit(solution)/shard_map/ppermute | solution.py:16
  151.1 11.6 %conditional.5 = ((f32[8,384,128]{2,1,0:T(8,128)}, f32[8,384]{1,0:T(8,128)S(1)})) conditional(s32[]{:T(128)} %bitcast.12, (f32[8,384,128]{2,1,0:T(8,128)}, f32[8,384]{1,0:T(8,128)S(1)}) %tuple.34, (s32[]{:T(128)}, s32[64,2]{0,1:T(2,128)S(1)}, s32[384]{0:T(512)S(1)}, pred[384]{0:T(512)(128)(4,1)S(1)}, s32[384]{0:T(512)S(1)}, ...), branch_computations={%region_11.12_spmd, %region_12.15_spmd} | conditional | flops 618149760 | bytes 29263224 | solution.py:95
  151.1 1.9 %copy.87 = bf16[2,384,1024]{1,2,0:T(8,128)(2,1)S(1)} copy(bf16[2,384,1024]{2,1,0:T(8,128)(2,1)} %get-tuple-element.258) | data formatting | bytes 3145728 | tf_op jit(solution)/shard_map
  153.0 1.0 fusion.77
  154.7 1.3 and_or_fusion.1
  156.0 1.4 fusion.26
  157.3 1.1 fusion.27
  158.5 4.3 %multiply_add_fusion.4 = f32[8,384,128]{2,1,0:T(8,128)} fusion(f32[8,384,128]{2,1,0:T(8,128)} %get-tuple-element.180, bf16[384,8,128]{0,2,1:T(8,128)(2,1)S(1)} %bitcast.75, f32[8,384,384]{1,2,0:T(8,128)S(1)} %get-tuple-element.289, f32[8,384]{1,0:T(8,128)S(1)} %get-tuple-element.288, pred[384]{0:T(512)(128)(4,1)S(1)} %and_or_fusion.1, ...), kind=kOutput, calls=%fused_computation.45 | convolution fusion | flops 307888128 | bytes 8688000 | tf_op jit(solution)/shard_map/cond/branch_1_fun/hqk,khd->hqd/dot_general | solution.py:39
  162.7 2.8 %fusion.50 = bf16[384,1024]{1,0:T(8,128)(2,1)} fusion(pred[384]{0:T(512)(128)(4,1)S(1)} %and_or_fusion.3, f32[8,384,128]{2,1,0:T(8,128)} %get-tuple-element.205, f32[8,384]{1,0:T(8,128)S(1)} %get-tuple-element.206), kind=kLoop, calls=%fused_computation.67 | loop fusion | flops 1179648 | bytes 2371968 | tf_op jit(solution)/shard_map/convert_element_type | solution.py:100
  (57 shorter events, 10.7 us)
Async XLA Ops:
  16.6 1.0 copy-start
  17.6 48.3 %copy-start.6 = (s32[1,4]{1,0:T(1,128)S(1)}, s32[1,4]{1,0:T(1,128)}, u32[]{:S(2)}) copy-start(s32[1,4]{1,0:T(1,128)} %param.19) | copy-start | bytes 52
  17.6 50.8 %copy-start.2 = (bf16[1,128,1024]{2,1,0:T(8,128)(2,1)S(1)}, bf16[1,128,1024]{2,1,0:T(8,128)(2,1)}, u32[]{:S(2)}) copy-start(bf16[1,128,1024]{2,1,0:T(8,128)(2,1)} %get-tuple-element.298) | copy-start | bytes 786436
  17.8 51.6 %copy-start.4 = (bf16[128,1024]{1,0:T(8,128)(2,1)S(1)}, bf16[128,1024]{1,0:T(8,128)(2,1)}, u32[]{:S(2)}) copy-start(bf16[128,1024]{1,0:T(8,128)(2,1)} %param.13) | copy-start | bytes 786436
  17.8 46.2 %collective-permute-start = (bf16[2,384,1024]{2,1,0:T(8,128)(2,1)S(1)}, bf16[2,384,1024]{2,1,0:T(8,128)(2,1)}, u32[]{:S(2)}, u32[]{:S(2)}) collective-permute-start(bf16[2,384,1024]{2,1,0:T(8,128)(2,1)S(1)} %pad_maximum_fusion), channel_id=1, source_target_pairs={{0,4},{4,8},{8,12},{12,16},{16,20},{20,24},{24,28},{28,32},{32,36}... | collective-permute-start | bytes 4718600 | tf_op jit(solution)/shard_map/ppermute | solution.py:16
  64.0 44.0 %collective-permute-start.1 = (bf16[2,384,1024]{2,1,0:T(8,128)(2,1)}, bf16[2,384,1024]{2,1,0:T(8,128)(2,1)}, u32[]{:S(2)}, u32[]{:S(2)}) collective-permute-start(bf16[2,384,1024]{2,1,0:T(8,128)(2,1)} %collective-permute-done), channel_id=1, source_target_pairs={{0,4},{4,8},{8,12},{12,16},{16,20},{20,24},{24,28},{28,32},{32,36}... | collective-permute-start | bytes 4718600 | tf_op jit(solution)/shard_map/ppermute | solution.py:16
  69.1 1.2 copy-start.1
  69.9 1.2 copy-start.5
  108.0 43.1 %collective-permute-start.2 = (bf16[2,384,1024]{2,1,0:T(8,128)(2,1)}, bf16[2,384,1024]{2,1,0:T(8,128)(2,1)}, u32[]{:S(2)}, u32[]{:S(2)}) collective-permute-start(bf16[2,384,1024]{2,1,0:T(8,128)(2,1)} %collective-permute-done.1), channel_id=1, source_target_pairs={{0,4},{4,8},{8,12},{12,16},{16,20},{20,24},{24,28},{28,32},{32,36}... | collective-permute-start | bytes 4718600 | tf_op jit(solution)/shard_map/ppermute | solution.py:16
  157.3 1.1 copy-start.3
where the time goes:
time: 166 us; the launch traced here: 165 us
  waiting for transfers between devices  92.9 us (56%)
  matrix products  25.2 us (15%)
  local copies, waits for them, and re-layouts  16.1 us (10%)
  other arithmetic  14.3 us (9%)
  starting transfers between devices  7.44 us (4%)
  blocking collectives  6.98 us (4%)
  between operations  2.19 us (1%)
    ppermute x3, waiting for transfers between devices, from_behind(): return lax.ppermute(value, axis, pairs)  92.9 us
    dot_general x4, matrix products, block_partial(): jnp.einsum('hqk,khd->hqd', weights, values, preferred_element_type=jnp.fl...  15.5 us
    ppermute x3, starting transfers between devices, from_behind(): return lax.ppermute(value, axis, pairs)  7.44 us
    all_gather x1, blocking collectives, body(): lax.all_gather(frame_features, 'tp', axis=0, tiled=True)  6.98 us
    another operation x3, local copies, waits for them, and re-layouts  5.62 us
    or x4, other arithmetic, live_slots(): return frame_live | text_live  5.08 us
    dot_general x4, matrix products, block_partial(): jnp.einsum('qhd,khd->hqk', queries, keys, preferred_element_type=jnp.floa...  5 us
    dot_general x1, matrix products, norm_project(): jnp.einsum('rv,vmc->rmc', normed.astype(jnp.bfloat16), weights, preferred...  4.67 us
  transfers between devices with their start and end apart: 3, of which 3 were waited for; matrix products, arithmetic and copies ran while one was open for 18% of the time, Pallas kernels for 0%

commit v1 on v0

v1 whole, which is shorter than its diff:
```python
import math

import jax
import jax.numpy as jnp
from jax import lax
from jax.experimental import pallas as pl
from jax.experimental.pallas import tpu as pltpu
from jax.sharding import PartitionSpec as P

HD = 128
FT = 64
REACH = 4
PAD = 8
ROWS = FT + PAD
NEG = -1e30
SCALE = 1.4426950408889634 / math.sqrt(HD)
LOW, HIGH = 2.0**-60, 2.0**100
VM = pl.BlockSpec(memory_space=pltpu.VMEM)
SM = pl.BlockSpec(memory_space=pltpu.SMEM)
F32 = jnp.float32
BF16 = jnp.bfloat16
PARAMS = pltpu.CompilerParams(vmem_limit_bytes=24 << 20)


def dot_nt(a, b):
    return lax.dot_general(a, b, (((1,), (1,)), ((), ())), preferred_element_type=F32)


def dot_nn(a, b):
    return lax.dot_general(a, b, (((1,), (0,)), ((), ())), preferred_element_type=F32)


def prep_kernel(slot_ref, feat_ref, out_ref):
    me = lax.axis_index("tp")
    slot = jnp.int32(0)
    for j in range(1, slot_ref.shape[1]):
        slot = jnp.where(slot_ref[0, j] == me, jnp.int32(j), slot)
    feats = feat_ref[...].astype(F32)
    normed = feats * lax.rsqrt(jnp.mean(feats * feats, axis=1, keepdims=True) + 1e-05)
    out_ref[:FT, :] = normed.astype(BF16)
    out_ref[FT:, :] = jnp.full((PAD, out_ref.shape[1]), slot.astype(F32), F32).astype(BF16)


def slot_of(pay):
    return jnp.max(pay[FT:ROWS, :128].astype(F32)).astype(jnp.int32)


def live_rows(shape, nf, nt, frames):
    row = lax.broadcasted_iota(jnp.int32, shape, 0)
    return (row < nf * FT) | ((row >= frames) & (row - frames < nt))


def key_block(counts_ref, mask_ref, d, which):
    b = lax.axis_index("blk")
    return jnp.where(mask_ref[0, d] > 0, counts_ref[which, jnp.maximum(b - d, 0)], 0)


def own_kernel(counts_ref, pay0, payx, payc, tq, tkv, w, q_out, acc, l_out, x, kbuf, vbuf):
    cap, width = tq.shape
    frames = x.shape[0]
    span = frames + cap
    b = lax.axis_index("blk")
    nf = counts_ref[0, b]
    nt = counts_ref[1, b]
    for pay in (pay0[...], payx[...], payc[0], payc[1]):
        x[pl.ds(pl.multiple_of(slot_of(pay) * FT, FT), FT), :] = pay[:FT]
    q_out[frames:, :] = tq[...]
    kbuf[frames:, :] = tkv[0]
    trow = lax.broadcasted_iota(jnp.int32, (cap, width), 0)
    vbuf[frames:, :] = jnp.where(trow < nt, tkv[1], jnp.zeros_like(tkv[1]))
    rows = x[...]
    half = width // 2
    frow = lax.broadcasted_iota(jnp.int32, (frames, half), 0)
    for n in range(2):
        c = slice(n * half, (n + 1) * half)
        q_out[:frames, c] = dot_nn(rows, w[0, :, c]).astype(BF16)
        kbuf[:frames, c] = dot_nn(rows, w[1, :, c]).astype(BF16)
        vbuf[:frames, c] = jnp.where(frow < nf * FT, dot_nn(rows, w[2, :, c]), 0.0).astype(BF16)
    ones = jnp.where(live_rows((span, HD), nf, nt, frames), 1.0, 0.0).astype(BF16)
    step = cap
    causal = lax.broadcasted_iota(jnp.int32, (step, step), 0) >= lax.broadcasted_iota(jnp.int32, (step, step), 1)
    for h in range(width // HD):
        cols = slice(h * HD, (h + 1) * HD)
        for lo in range(0, span, step):
            hi = lo + step
            p = jnp.exp2(dot_nt(q_out[lo:hi, cols], kbuf[:hi, cols]) * SCALE)
            diag = jnp.where(causal, p[:, lo:hi], 0.0)
            p = jnp.concatenate([p[:, :lo], diag], axis=1) if lo else diag
            o = dot_nn(p.astype(BF16), jnp.concatenate([vbuf[:hi, cols], ones[:hi]], axis=1))
            acc[lo:hi, cols] = o[:, :HD]
            l_out[lo:hi, cols] = o[:, HD:]


def frames_kernel(counts_ref, mask_ref, p1, p3, p2, x13, x2, c13, c2, q, w, acc_in, l_in, acc, l, x, kbuf, vbuf):
    width = q.shape[1]
    part = kbuf.shape[0]
    n = jnp.int32(0)
    groups = {
        1: (p1[...], x13[0], c13[0], c13[2]),
        2: (p2[...], x2[...], c2[0], c2[1]),
        3: (p3[...], x13[1], c13[1], c13[3]),
    }
    for d in range(1, REACH):
        nf = key_block(counts_ref, mask_ref, d, 0)
        for pay in groups[d]:
            x[pl.ds(pl.multiple_of(n * FT, FT), FT), :] = pay[:FT]
            n = n + (slot_of(pay) < nf).astype(jnp.int32)
    for j in range(part // FT):
        x[pl.ds(pl.multiple_of((n + j) * FT, FT), FT), :] = jnp.zeros((FT, x.shape[1]), BF16)

    def step(c, _):
        rows = x[pl.ds(pl.multiple_of(c * part, part), part), :]
        kbuf[...] = dot_nn(rows, w[1]).astype(BF16)
        vbuf[...] = dot_nn(rows, w[2]).astype(BF16)
        row = lax.broadcasted_iota(jnp.int32, (part, HD), 0)
        ones = jnp.where(row < n * FT - c * part, 1.0, 0.0).astype(BF16)
        for h in range(width // HD):
            cols = slice(h * HD, (h + 1) * HD)
            p = jnp.exp2(dot_nt(q[:, cols], kbuf[:, cols]) * SCALE).astype(BF16)
            o = dot_nn(p, jnp.concatenate([vbuf[:, cols], ones], axis=1))
            acc[:, cols] += o[:, :HD]
            l[:, cols] += o[:, HD:]
        return 0

    lax.fori_loop(0, (n * FT + part - 1) // part, step, 0)


def text_kernel(counts_ref, mask_ref, t1, t2, t3, q, acc, l, out, bad):
    span, width = q.shape
    cap = t1.shape[1]
    b = lax.axis_index("blk")
    row = lax.broadcasted_iota(jnp.int32, (cap, HD), 0)
    ones = jnp.concatenate(
        [jnp.where(row < key_block(counts_ref, mask_ref, d, 1), 1.0, 0.0).astype(BF16) for d in range(1, REACH)], axis=0
    )
    live = live_rows((span, HD), counts_ref[0, b], counts_ref[1, b], span - cap)
    worst = jnp.zeros((span, HD), F32)
    for h in range(width // HD):
        cols = slice(h * HD, (h + 1) * HD)
        keys = jnp.concatenate([t[0, :, cols] for t in (t1, t2, t3)], axis=0)
        values = jnp.concatenate([t[1, :, cols] for t in (t1, t2, t3)], axis=0) * ones
        p = jnp.exp2(dot_nt(q[:, cols], keys) * SCALE).astype(BF16)
        o = dot_nn(p, jnp.concatenate([values, ones], axis=1))
        s = l[:, cols] + o[:, HD:]
        worst = jnp.where((s > LOW) & (s < HIGH), worst, 1.0)
        out[:, cols] = jnp.where(live, (acc[:, cols] + o[:, :HD]) / s, 0.0).astype(BF16)
    bad[...] = jnp.max(jnp.where(live, worst, 0.0), axis=0, keepdims=True)


def exact_kernel(
    counts_ref, mask_ref, pay0, payx, payc, p1, p3, p2, x13, x2, c13, c2, tkv, t1, t2, t3, q, w, out,
    x, text, kbuf, vbuf, acc, m_all, l_all
):
    span, width = q.shape
    cap = tkv.shape[1]
    frames = span - cap
    b = lax.axis_index("blk")
    groups = (
        (pay0[...], payx[...], payc[0], payc[1]),
        (p1[...], x13[0], c13[0], c13[2]),
        (p2[...], x2[...], c2[0], c2[1]),
        (p3[...], x13[1], c13[1], c13[3]),
    )
    for d, texts in enumerate((tkv, t1, t2, t3)):
        for pay in groups[d]:
            x[pl.ds(pl.multiple_of(d * frames + slot_of(pay) * FT, FT), FT), :] = pay[:FT]
        text[d] = texts[...]
    acc[...] = jnp.zeros_like(acc)
    m_all[...] = jnp.full_like(m_all, NEG)
    l_all[...] = jnp.zeros_like(l_all)
    lane = lax.broadcasted_iota(jnp.int32, (span, HD), 1)
    qpos = lax.broadcasted_iota(jnp.int32, (span, span), 0)
    kpos = lax.broadcasted_iota(jnp.int32, (span, span), 1)

    def block(d, _):
        nf = counts_ref[0, jnp.maximum(b - d, 0)]
        nt = counts_ref[1, jnp.maximum(b - d, 0)]

        @pl.when(mask_ref[0, d] > 0)
        def _():
            rows = x[pl.ds(pl.multiple_of(d * frames, frames), frames), :]
            kbuf[:frames, :] = dot_nn(rows, w[1]).astype(BF16)
            vbuf[:frames, :] = dot_nn(rows, w[2]).astype(BF16)
            kbuf[frames:, :] = text[d, 0]
            vbuf[frames:, :] = text[d, 1]
            allowed = (kpos < nf * FT) | ((kpos >= frames) & (kpos - frames < nt))
            allowed = allowed & ((qpos >= kpos) | (jnp.zeros_like(kpos) + d > 0))
            bias = jnp.where(allowed, 0.0, NEG)

            def head(h, _):
                cols = pl.ds(pl.multiple_of(h * HD, HD), HD)
                old = jnp.max(jnp.where(lane == h, m_all[...], NEG), axis=1, keepdims=True)
                s = dot_nt(q[:, cols], kbuf[:, cols]) * SCALE + bias
                top = jnp.maximum(jnp.max(s, axis=1, keepdims=True), old)
                p = jnp.exp2(s - top)
                keep = jnp.exp2(old - top)
                acc[:, cols] = acc[:, cols] * keep + dot_nn(p.astype(BF16), vbuf[:, cols])
                total = jnp.sum(p, axis=1, keepdims=True)
                l_all[...] = jnp.where(lane == h, l_all[...] * keep + total, l_all[...])
                m_all[...] = jnp.where(lane == h, top, m_all[...])
                return 0

            lax.fori_loop(0, width // HD, head, 0)

        return 0

    lax.fori_loop(0, REACH, block, 0)
    live = live_rows((span, HD), counts_ref[0, b], counts_ref[1, b], frames)

    def finish(h, _):
        cols = pl.ds(pl.multiple_of(h * HD, HD), HD)
        total = jnp.max(jnp.where(lane == h, l_all[...], 0.0), axis=1, keepdims=True)
        out[:, cols] = jnp.where(live, acc[:, cols] / total, 0.0).astype(BF16)
        return 0

    lax.fori_loop(0, width // HD, finish, 0)


def shift(value, by):
    length = lax.axis_size("blk")
    return lax.ppermute(value, "blk", [(i, (i + by) % length) for i in range(length)])


def across(value, bit):
    return lax.ppermute(value, "tp", [(i, i ^ bit) for i in range(lax.axis_size("tp"))])


def after(value, *others):
    return lax.optimization_barrier((value, *others))


def body(text_query, text_keyval, frame_features, frame_proj, frame_slot, counts, block_mask):
    cap, width = text_query.shape
    frames = frame_slot.shape[1] * FT
    span = frames + cap
    vw = frame_features.shape[1]
    weights = jnp.transpose(frame_proj, (1, 0, 2))
    counts = counts.T
    pay = pl.pallas_call(
        prep_kernel,
        out_shape=jax.ShapeDtypeStruct((ROWS, vw), BF16),
        in_specs=[SM, VM],
        out_specs=VM,
        compiler_params=PARAMS,
        name="prep",
    )(frame_slot, frame_features)
    p3 = shift(pay, 3)
    p1 = shift(pay, 1)
    own_x = across(pay, 2)
    p1, p3, own_x, kv = after(p1, p3, own_x, text_keyval)
    own_c = across(jnp.stack([pay, own_x]), 1)
    pair = jnp.stack([p1, p3])
    x13 = across(pair, 2)
    p2 = shift(p3, -1)
    t3 = shift(kv, 3)
    t1 = shift(kv, 1)
    sums = jax.ShapeDtypeStruct((span, width), F32)
    q, acc, l = pl.pallas_call(
        own_kernel,
        out_shape=(jax.ShapeDtypeStruct((span, width), BF16), sums, sums),
        in_specs=[SM] + [VM] * 6,
        out_specs=(VM,) * 3,
        scratch_shapes=[
            pltpu.VMEM((frames, vw), BF16),
            pltpu.VMEM((span, width), BF16),
            pltpu.VMEM((span, width), BF16),
        ],
        compiler_params=PARAMS,
        name="own",
    )(counts, pay, own_x, own_c, text_query, text_keyval, weights)
    acc, p2, x13, t3 = after(acc, p2, x13, t3)
    x2 = across(p2, 2)
    c13 = across(jnp.concatenate([pair, x13]), 1)
    c2 = across(jnp.stack([p2, x2]), 1)
    t2 = shift(t3, -1)
    acc, l = pl.pallas_call(
        frames_kernel,
        out_shape=(sums, sums),
        in_specs=[SM, SM] + [VM] * 11,
        out_specs=(VM,) * 2,
        input_output_aliases={11: 0, 12: 1},
        scratch_shapes=[
            pltpu.VMEM((4 * frames, vw), BF16),
            pltpu.VMEM((frames, width), BF16),
            pltpu.VMEM((frames, width), BF16),
        ],
        compiler_params=PARAMS,
        name="frames",
    )(counts, block_mask, p1, p3, p2, x13, x2, c13, c2, q, weights, acc, l)
    out, bad = pl.pallas_call(
        text_kernel,
        out_shape=(jax.ShapeDtypeStruct((span, width), BF16), jax.ShapeDtypeStruct((1, HD), F32)),
        in_specs=[SM, SM] + [VM] * 6,
        out_specs=(VM, VM),
        compiler_params=PARAMS,
        name="text",
    )(counts, block_mask, t1, t2, t3, q, acc, l)

    def exact():
        return pl.pallas_call(
            exact_kernel,
            out_shape=jax.ShapeDtypeStruct((span, width), BF16),
            in_specs=[SM, SM] + [VM] * 16,
            out_specs=VM,
            scratch_shapes=[
                pltpu.VMEM((REACH * frames, vw), BF16),
                pltpu.VMEM((REACH, 2, cap, width), BF16),
                pltpu.VMEM((span, width), BF16),
                pltpu.VMEM((span, width), BF16),
                pltpu.VMEM((span, width), F32),
                pltpu.VMEM((span, HD), F32),
                pltpu.VMEM((span, HD), F32),
            ],
            compiler_params=pltpu.CompilerParams(vmem_limit_bytes=48 << 20),
            name="exact",
        )(
            counts, block_mask, pay, own_x, own_c, p1, p3, p2, x13, x2, c13, c2,
            text_keyval, t1, t2, t3, q, weights
        )

    return lax.cond(jnp.max(bad) > 0, exact, lambda: out)


def solution(mesh):
    placed = (
        P("blk", "tp"),
        P(None, "blk", "tp"),
        P(("blk", "tp"), None),
        P(None, None, "tp"),
        P("blk", None),
        P(),
        P("blk", None),
    )
    return jax.shard_map(
        body, mesh=mesh, in_specs=placed, out_specs=P("blk", "tp"), check_vma=False
    )
```

time: 166 us -> 85.9 us (0.52)
  the two profiles are of different devices: /device:TPU:6 before, /device:TPU:124 now
where the time goes in v1:
time: 85.9 us; the launch traced here: 86.8 us
  Pallas kernels  43.9 us (51%)
  waiting for transfers between devices  21.1 us (25%)
  starting transfers between devices  18.5 us (22%)
  local copies, waits for them, and re-layouts  1.64 us (2%)
    pallas_call x1, Pallas kernels, exact(): pl.pallas_call(exact_kernel, out_shape=jax.ShapeDtypeStruct((span, width)...  27 us
    ppermute x6, waiting for transfers between devices, shift(): lax.ppermute(value, 'blk', [(i, (i + by) % length) for i in range(length)])  18.9 us
    ppermute x6, starting transfers between devices, shift(): lax.ppermute(value, 'blk', [(i, (i + by) % length) for i in range(length)])  14.9 us
    pallas_call x1, Pallas kernels, body(): pl.pallas_call(own_kernel, out_shape=(jax.ShapeDtypeStruct((span, width),...  7.76 us
    pallas_call x1, Pallas kernels, body(): pl.pallas_call(frames_kernel, out_shape=(sums, sums), in_specs=[SM, SM] +...  5.27 us
    ppermute x6, starting transfers between devices, across(): lax.ppermute(value, 'tp', [(i, i ^ bit) for i in range(lax.axis_size('tp'...  3.57 us
    pallas_call x1, Pallas kernels, body(): pl.pallas_call(text_kernel, out_shape=(jax.ShapeDtypeStruct((span, width)...  3.23 us
    ppermute x6, waiting for transfers between devices, across(): lax.ppermute(value, 'tp', [(i, i ^ bit) for i in range(lax.axis_size('tp'...  2.19 us
  transfers between devices with their start and end apart: 12, of which 8 were waited for; matrix products, arithmetic and copies ran while one was open for 0% of the time, Pallas kernels for 15%

profile of v1, /device:TPU:124, one launch (start us, length us, event | category | flops | bytes accessed | tf_op | source)
XLA Modules:
  0.0 86.8 jit_solution(13985561283680757218)
XLA Ops:
  0.0 0.9 %copy-done.1 = bf16[64,1024]{1,0:T(8,128)(2,1)S(1)} copy-done((bf16[64,1024]{1,0:T(8,128)(2,1)S(1)}, bf16[64,1024]{1,0:T(8,128)(2,1)}, u32[]{:S(2)}) %copy-start.1) | copy-done | bytes 131096
  1.0 0.7 copy-done.2
  1.6 0.7 prep.1.pay0
  2.3 1.3 %collective-permute-start.2 = (bf16[72,1024]{1,0:T(8,128)(2,1)S(1)}, bf16[72,1024]{1,0:T(8,128)(2,1)S(1)}, u32[]{:S(2)}, u32[]{:S(2)}) collective-permute-start(bf16[72,1024]{1,0:T(8,128)(2,1)S(1)} %prep.1.pay0), channel_id=1, source_target_pairs={{0,2},{1,3},{2,0},{3,1},{4,6},{5,7},{6,4},{7,5},{8,10},{9,11},{10,... | collective-permute-start | bytes 442376 | tf_op jit(solution)/shard_map/ppermute | solution.py:225
  3.6 3.3 %collective-permute-start.1 = (bf16[72,1024]{1,0:T(8,128)(2,1)S(1)}, bf16[72,1024]{1,0:T(8,128)(2,1)S(1)}, u32[]{:S(2)}, u32[]{:S(2)}) collective-permute-start(bf16[72,1024]{1,0:T(8,128)(2,1)S(1)} %prep.1.pay0), channel_id=1, source_target_pairs={{0,12},{4,16},{8,20},{12,24},{16,28},{20,32},{24,36},{28,40},{32,4... | collective-permute-start | bytes 442376 | tf_op jit(solution)/shard_map/ppermute | solution.py:221
  6.9 2.5 %collective-permute-start = (bf16[72,1024]{1,0:T(8,128)(2,1)S(1)}, bf16[72,1024]{1,0:T(8,128)(2,1)S(1)}, u32[]{:S(2)}, u32[]{:S(2)}) collective-permute-start(bf16[72,1024]{1,0:T(8,128)(2,1)S(1)} %prep.1.pay0), channel_id=1, source_target_pairs={{0,4},{4,8},{8,12},{12,16},{16,20},{20,24},{24,28},{28,32},{32,36}... | collective-permute-start | bytes 442376 | tf_op jit(solution)/shard_map/ppermute | solution.py:221
  9.4 1.3 %collective-permute-done.1.p3 = bf16[72,1024]{1,0:T(8,128)(2,1)S(1)} collective-permute-done((bf16[72,1024]{1,0:T(8,128)(2,1)S(1)}, bf16[72,1024]{1,0:T(8,128)(2,1)S(1)}, u32[]{:S(2)}, u32[]{:S(2)}) %collective-permute-start.1) | collective-permute-done | bytes 147488 | tf_op jit(solution)/shard_map/ppermute | solution.py:221
  10.7 2.2 %collective-permute-done.p1 = bf16[72,1024]{1,0:T(8,128)(2,1)S(1)} collective-permute-done((bf16[72,1024]{1,0:T(8,128)(2,1)S(1)}, bf16[72,1024]{1,0:T(8,128)(2,1)S(1)}, u32[]{:S(2)}, u32[]{:S(2)}) %collective-permute-start) | collective-permute-done | bytes 147488 | tf_op jit(solution)/shard_map/ppermute | solution.py:221
  12.8 2.4 %collective-permute-start.7 = (bf16[2,128,1024]{2,1,0:T(8,128)(2,1)}, bf16[2,128,1024]{2,1,0:T(8,128)(2,1)S(1)}, u32[]{:S(2)}, u32[]{:S(2)}) collective-permute-start(bf16[2,128,1024]{2,1,0:T(8,128)(2,1)} %tkv.1), channel_id=1, source_target_pairs={{0,12},{4,16},{8,20},{12,24},{16,28},{20,32},{24,36},{28,40},{32,4... | collective-permute-start | bytes 1572872 | tf_op jit(solution)/shard_map/ppermute | solution.py:221
  15.3 0.1 collective-permute-start.4
  15.4 0.9 %collective-permute-start.6 = (bf16[2,72,1024]{2,1,0:T(8,128)(2,1)S(1)}, bf16[2,72,1024]{2,1,0:T(8,128)(2,1)S(1)}, u32[]{:S(2)}, u32[]{:S(2)}) collective-permute-start(bf16[2,72,1024]{2,1,0:T(8,128)(2,1)S(1)} %pad_maximum_fusion.2), channel_id=1, source_target_pairs={{0,2},{1,3},{2,0},{3,1},{4,6},{5,7},{6,4},{7,5},{8,10},{9,11},{10,... | collective-permute-start | bytes 884744 | tf_op jit(solution)/shard_map/ppermute | solution.py:225
  16.4 0.6 collective-permute-done.4.payc
  17.0 7.8 %own.1 = (bf16[384,1024]{1,0:T(8,128)(2,1)S(1)}, f32[384,1024]{1,0:T(8,128)S(1)}, f32[384,1024]{1,0:T(8,128)S(1)}) custom-call(s32[2,64]{1,0:T(2,128)} %bitcast.19, bf16[72,1024]{1,0:T(8,128)(2,1)S(1)} %prep.1.pay0, bf16[72,1024]{1,0:T(8,128)(2,1)S(1)} %collective-permute-done.2.payx, bf16[2,72,1024]{2,1,0:T(8,128)(2,1)S(1)} %collective-permute-done.4.payc, ...), custom_call_target="tpu_custom_call" | custom-call | tf_op jit(solution)/shard_map/own/pallas_call | solution.py:258
  24.8 0.0 copy-start.10
  24.8 0.0 copy-start.11
  24.8 1.7 %collective-permute-done.5.p2 = bf16[72,1024]{1,0:T(8,128)(2,1)S(1)} collective-permute-done((bf16[72,1024]{1,0:T(8,128)(2,1)S(1)}, bf16[72,1024]{1,0:T(8,128)(2,1)S(1)}, u32[]{:S(2)}, u32[]{:S(2)}) %collective-permute-start.5) | collective-permute-done | bytes 147488 | tf_op jit(solution)/shard_map/ppermute | solution.py:221
  26.5 0.0 collective-permute-done.6.x13
  26.5 3.9 %collective-permute-done.7.t3 = bf16[2,128,1024]{2,1,0:T(8,128)(2,1)S(1)} collective-permute-done((bf16[2,128,1024]{2,1,0:T(8,128)(2,1)}, bf16[2,128,1024]{2,1,0:T(8,128)(2,1)S(1)}, u32[]{:S(2)}, u32[]{:S(2)}) %collective-permute-start.7) | collective-permute-done | bytes 524320 | tf_op jit(solution)/shard_map/ppermute | solution.py:221
  30.4 0.1 pad_maximum_fusion
  30.5 0.1 collective-permute-start.10
  30.6 0.9 %collective-permute-start.9 = (bf16[72,1024]{1,0:T(8,128)(2,1)S(1)}, bf16[72,1024]{1,0:T(8,128)(2,1)S(1)}, u32[]{:S(2)}, u32[]{:S(2)}) collective-permute-start(bf16[72,1024]{1,0:T(8,128)(2,1)S(1)} %collective-permute-done.5.p2), channel_id=1, source_target_pairs={{0,2},{1,3},{2,0},{3,1},{4,6},{5,7},{6,4},{7,5},{8,10},{9,11},{10,... | collective-permute-start | bytes 442376 | tf_op jit(solution)/shard_map/ppermute | solution.py:225
  31.5 6.7 %collective-permute-start.3 = (bf16[2,128,1024]{2,1,0:T(8,128)(2,1)S(1)}, bf16[2,128,1024]{2,1,0:T(8,128)(2,1)S(1)}, u32[]{:S(2)}, u32[]{:S(2)}) collective-permute-start(bf16[2,128,1024]{2,1,0:T(8,128)(2,1)S(1)} %copy-done.4), channel_id=1, source_target_pairs={{0,4},{4,8},{8,12},{12,16},{16,20},{20,24},{24,28},{28,32},{32,36}... | collective-permute-start | bytes 1572872 | tf_op jit(solution)/shard_map/ppermute | solution.py:221
  38.2 0.0 collective-permute-start.8
  38.2 0.3 collective-permute-start.11
  38.5 1.6 %collective-permute-done.11.c2 = bf16[2,72,1024]{2,1,0:T(8,128)(2,1)S(1)} collective-permute-done((bf16[2,72,1024]{2,1,0:T(8,128)(2,1)S(1)}, bf16[2,72,1024]{2,1,0:T(8,128)(2,1)S(1)}, u32[]{:S(2)}, u32[]{:S(2)}) %collective-permute-start.11) | collective-permute-done | bytes 294944 | tf_op jit(solution)/shard_map/ppermute | solution.py:225
  40.1 5.3 %frames.1 = (f32[384,1024]{1,0:T(8,128)S(1)}, f32[384,1024]{1,0:T(8,128)S(1)}) custom-call(s32[2,64]{1,0:T(2,128)S(1)} %bitcast.20, s32[1,4]{1,0:T(1,128)S(1)} %copy-done.11, bf16[72,1024]{1,0:T(8,128)(2,1)S(1)} %collective-permute-done.p1, bf16[72,1024]{1,0:T(8,128)(2,1)S(1)} %collective-permute-done.1.p3, ...), custom_call_target="tpu_custom_call", output_to_operand_aliasing={{0}: (11, {}), {1}: (12, {})} | custom-call | tf_op jit(solution)/shard_map/frames/pallas_call | solution.py:276
  45.4 4.3 %collective-permute-done.3.t1 = bf16[2,128,1024]{2,1,0:T(8,128)(2,1)S(1)} collective-permute-done((bf16[2,128,1024]{2,1,0:T(8,128)(2,1)S(1)}, bf16[2,128,1024]{2,1,0:T(8,128)(2,1)S(1)}, u32[]{:S(2)}, u32[]{:S(2)}) %collective-permute-start.3) | collective-permute-done | bytes 524320 | tf_op jit(solution)/shard_map/ppermute | solution.py:221
  49.7 5.5 %collective-permute-done.8.t2 = bf16[2,128,1024]{2,1,0:T(8,128)(2,1)S(1)} collective-permute-done((bf16[2,128,1024]{2,1,0:T(8,128)(2,1)S(1)}, bf16[2,128,1024]{2,1,0:T(8,128)(2,1)S(1)}, u32[]{:S(2)}, u32[]{:S(2)}) %collective-permute-start.8) | collective-permute-done | bytes 524320 | tf_op jit(solution)/shard_map/ppermute | solution.py:221
  55.2 3.2 %text.1 = (bf16[384,1024]{1,0:T(8,128)(2,1)}, f32[1,128]{1,0:T(1,128)S(1)}) custom-call(s32[2,64]{1,0:T(2,128)S(1)} %bitcast.21, s32[1,4]{1,0:T(1,128)S(1)} %copy-done.11, bf16[2,128,1024]{2,1,0:T(8,128)(2,1)S(1)} %collective-permute-done.3.t1, bf16[2,128,1024]{2,1,0:T(8,128)(2,1)S(1)} %collective-permute-done.8.t2, ...), custom_call_target="tpu_custom_call" | custom-call | tf_op jit(solution)/shard_map/text/pallas_call | solution.py:290
  58.4 0.7 reduce_max.9
  59.8 27.0 %conditional.1 = (bf16[384,1024]{1,0:T(8,128)(2,1)}) conditional(s32[]{:T(128)} %convert_element_type.3, bf16[384,1024]{1,0:T(8,128)(2,1)} %get-tuple-element.92, (s32[2,64]{1,0:T(2,128)S(1)}, s32[1,4]{1,0:T(1,128)S(1)}, bf16[72,1024]{1,0:T(8,128)(2,1)S(1)}, bf16[72,1024]{1,0:T(8,128)(2,1)S(1)}, bf16[2,72,1024]{2,1,0:T(8,128)(2,1)}, ...), branch_computations={%region_1.0_spmd, %region_2.0_spmd} | conditional | bytes 8 | solution.py:321
  59.8 27.0 %exact.1 = bf16[384,1024]{1,0:T(8,128)(2,1)} custom-call(s32[2,64]{1,0:T(2,128)S(1)} %get-tuple-element.45.counts_ref, s32[1,4]{1,0:T(1,128)S(1)} %get-tuple-element.46.mask_ref, bf16[72,1024]{1,0:T(8,128)(2,1)S(1)} %get-tuple-element.47.pay0, bf16[72,1024]{1,0:T(8,128)(2,1)S(1)} %get-tuple-element.48.payx, bf16[2,72,1024]{2,1,0:T(8,128)(2,1)} %get-tuple-element.49.payc, ...), custom_call_target="tpu_custom_call" | custom-call | tf_op jit(solution)/shard_map/cond/branch_1_fun/exact/pallas_call | solution.py:300
  (27 shorter events, 0.1 us)
Async XLA Ops:
  0.0 17.0 %copy-start = (bf16[128,1024]{1,0:T(8,128)(2,1)S(1)}, bf16[128,1024]{1,0:T(8,128)(2,1)}, u32[]{:S(2)}) copy-start(bf16[128,1024]{1,0:T(8,128)(2,1)} %tq.1) | copy-start | bytes 786436
  0.0 0.9 %copy-start.1 = (bf16[64,1024]{1,0:T(8,128)(2,1)S(1)}, bf16[64,1024]{1,0:T(8,128)(2,1)}, u32[]{:S(2)}) copy-start(bf16[64,1024]{1,0:T(8,128)(2,1)} %feat_ref.1) | copy-start | bytes 393220
  1.0 0.7 copy-start.2
  1.6 15.4 %copy-start.4 = (bf16[2,128,1024]{2,1,0:T(8,128)(2,1)S(1)}, bf16[2,128,1024]{2,1,0:T(8,128)(2,1)}, u32[]{:S(2)}) copy-start(bf16[2,128,1024]{2,1,0:T(8,128)(2,1)} %tkv.1) | copy-start | bytes 1572868
  2.3 7.1 %collective-permute-start.2 = (bf16[72,1024]{1,0:T(8,128)(2,1)S(1)}, bf16[72,1024]{1,0:T(8,128)(2,1)S(1)}, u32[]{:S(2)}, u32[]{:S(2)}) collective-permute-start(bf16[72,1024]{1,0:T(8,128)(2,1)S(1)} %prep.1.pay0), channel_id=1, source_target_pairs={{0,2},{1,3},{2,0},{3,1},{4,6},{5,7},{6,4},{7,5},{8,10},{9,11},{10,... | collective-permute-start | bytes 442376 | tf_op jit(solution)/shard_map/ppermute | solution.py:225
  3.6 7.1 %collective-permute-start.1 = (bf16[72,1024]{1,0:T(8,128)(2,1)S(1)}, bf16[72,1024]{1,0:T(8,128)(2,1)S(1)}, u32[]{:S(2)}, u32[]{:S(2)}) collective-permute-start(bf16[72,1024]{1,0:T(8,128)(2,1)S(1)} %prep.1.pay0), channel_id=1, source_target_pairs={{0,12},{4,16},{8,20},{12,24},{16,28},{20,32},{24,36},{28,40},{32,4... | collective-permute-start | bytes 442376 | tf_op jit(solution)/shard_map/ppermute | solution.py:221
  6.9 6.0 %collective-permute-start = (bf16[72,1024]{1,0:T(8,128)(2,1)S(1)}, bf16[72,1024]{1,0:T(8,128)(2,1)S(1)}, u32[]{:S(2)}, u32[]{:S(2)}) collective-permute-start(bf16[72,1024]{1,0:T(8,128)(2,1)S(1)} %prep.1.pay0), channel_id=1, source_target_pairs={{0,4},{4,8},{8,12},{12,16},{16,20},{20,24},{24,28},{28,32},{32,36}... | collective-permute-start | bytes 442376 | tf_op jit(solution)/shard_map/ppermute | solution.py:221
  12.8 17.5 %collective-permute-start.7 = (bf16[2,128,1024]{2,1,0:T(8,128)(2,1)}, bf16[2,128,1024]{2,1,0:T(8,128)(2,1)S(1)}, u32[]{:S(2)}, u32[]{:S(2)}) collective-permute-start(bf16[2,128,1024]{2,1,0:T(8,128)(2,1)} %tkv.1), channel_id=1, source_target_pairs={{0,12},{4,16},{8,20},{12,24},{16,28},{20,32},{24,36},{28,40},{32,4... | collective-permute-start | bytes 1572872 | tf_op jit(solution)/shard_map/ppermute | solution.py:221
  15.3 1.7 %collective-permute-start.4 = (bf16[2,72,1024]{2,1,0:T(8,128)(2,1)S(1)}, bf16[2,72,1024]{2,1,0:T(8,128)(2,1)S(1)}, u32[]{:S(2)}, u32[]{:S(2)}) collective-permute-start(bf16[2,72,1024]{2,1,0:T(8,128)(2,1)S(1)} %pad_maximum_fusion.1), channel_id=1, source_target_pairs={{0,1},{1,0},{2,3},{3,2},{4,5},{5,4},{6,7},{7,6},{8,9},{9,8},{10,11... | collective-permute-start | bytes 884744 | tf_op jit(solution)/shard_map/ppermute | solution.py:225
  15.4 11.1 %collective-permute-start.6 = (bf16[2,72,1024]{2,1,0:T(8,128)(2,1)S(1)}, bf16[2,72,1024]{2,1,0:T(8,128)(2,1)S(1)}, u32[]{:S(2)}, u32[]{:S(2)}) collective-permute-start(bf16[2,72,1024]{2,1,0:T(8,128)(2,1)S(1)} %pad_maximum_fusion.2), channel_id=1, source_target_pairs={{0,2},{1,3},{2,0},{3,1},{4,6},{5,7},{6,4},{7,5},{8,10},{9,11},{10,... | collective-permute-start | bytes 884744 | tf_op jit(solution)/shard_map/ppermute | solution.py:225
  16.3 10.2 %collective-permute-start.5 = (bf16[72,1024]{1,0:T(8,128)(2,1)S(1)}, bf16[72,1024]{1,0:T(8,128)(2,1)S(1)}, u32[]{:S(2)}, u32[]{:S(2)}) collective-permute-start(bf16[72,1024]{1,0:T(8,128)(2,1)S(1)} %collective-permute-done.1.p3), channel_id=1, source_target_pairs={{0,252},{4,0},{8,4},{12,8},{16,12},{20,16},{24,20},{28,24},{32,28}... | collective-permute-start | bytes 442376 | tf_op jit(solution)/shard_map/ppermute | solution.py:221
  17.0 7.8 %copy-start.8 = (bf16[2,72,1024]{2,1,0:T(8,128)(2,1)}, bf16[2,72,1024]{2,1,0:T(8,128)(2,1)S(1)}, u32[]{:S(2)}) copy-start(bf16[2,72,1024]{2,1,0:T(8,128)(2,1)S(1)} %collective-permute-done.4.payc) | copy-start | bytes 884740
  17.0 23.1 %copy-start.3 = (bf16[1024,3,1024]{2,0,1:T(8,128)(2,1)S(1)}, bf16[1024,3,1024]{2,0,1:T(8,128)(2,1)}, u32[]{:S(2)}) copy-start(bf16[1024,3,1024]{2,0,1:T(8,128)(2,1)} %param.12) | copy-start | bytes 18874372
  24.8 15.3 %copy-start.10 = (s32[64,2]{0,1:T(2,128)S(1)}, s32[64,2]{0,1:T(2,128)}, u32[]{:S(2)}) copy-start(s32[64,2]{0,1:T(2,128)} %param.14) | copy-start | bytes 1540
  24.8 15.3 %copy-start.11 = (s32[1,4]{1,0:T(1,128)S(1)}, s32[1,4]{1,0:T(1,128)}, u32[]{:S(2)}) copy-start(s32[1,4]{1,0:T(1,128)} %mask_ref.3) | copy-start | bytes 52
  30.5 9.6 %collective-permute-start.10 = (bf16[4,72,1024]{2,1,0:T(8,128)(2,1)S(1)}, bf16[4,72,1024]{2,1,0:T(8,128)(2,1)S(1)}, u32[]{:S(2)}, u32[]{:S(2)}) collective-permute-start(bf16[4,72,1024]{2,1,0:T(8,128)(2,1)S(1)} %pad_maximum_fusion), channel_id=1, source_target_pairs={{0,1},{1,0},{2,3},{3,2},{4,5},{5,4},{6,7},{7,6},{8,9},{9,8},{10,11... | collective-permute-start | bytes 1769480 | tf_op jit(solution)/shard_map/ppermute | solution.py:225
  30.6 7.6 %collective-permute-start.9 = (bf16[72,1024]{1,0:T(8,128)(2,1)S(1)}, bf16[72,1024]{1,0:T(8,128)(2,1)S(1)}, u32[]{:S(2)}, u32[]{:S(2)}) collective-permute-start(bf16[72,1024]{1,0:T(8,128)(2,1)S(1)} %collective-permute-done.5.p2), channel_id=1, source_target_pairs={{0,2},{1,3},{2,0},{3,1},{4,6},{5,7},{6,4},{7,5},{8,10},{9,11},{10,... | collective-permute-start | bytes 442376 | tf_op jit(solution)/shard_map/ppermute | solution.py:225
  31.5 18.2 %collective-permute-start.3 = (bf16[2,128,1024]{2,1,0:T(8,128)(2,1)S(1)}, bf16[2,128,1024]{2,1,0:T(8,128)(2,1)S(1)}, u32[]{:S(2)}, u32[]{:S(2)}) collective-permute-start(bf16[2,128,1024]{2,1,0:T(8,128)(2,1)S(1)} %copy-done.4), channel_id=1, source_target_pairs={{0,4},{4,8},{8,12},{12,16},{16,20},{20,24},{24,28},{28,32},{32,36}... | collective-permute-start | bytes 1572872 | tf_op jit(solution)/shard_map/ppermute | solution.py:221
  38.2 17.0 %collective-permute-start.8 = (bf16[2,128,1024]{2,1,0:T(8,128)(2,1)S(1)}, bf16[2,128,1024]{2,1,0:T(8,128)(2,1)S(1)}, u32[]{:S(2)}, u32[]{:S(2)}) collective-permute-start(bf16[2,128,1024]{2,1,0:T(8,128)(2,1)S(1)} %collective-permute-done.7.t3), channel_id=1, source_target_pairs={{0,252},{4,0},{8,4},{12,8},{16,12},{20,16},{24,20},{28,24},{32,28}... | collective-permute-start | bytes 1572872 | tf_op jit(solution)/shard_map/ppermute | solution.py:221
  38.2 7.2 %copy-start.7 = (bf16[72,1024]{1,0:T(8,128)(2,1)}, bf16[72,1024]{1,0:T(8,128)(2,1)S(1)}, u32[]{:S(2)}) copy-start(bf16[72,1024]{1,0:T(8,128)(2,1)S(1)} %collective-permute-done.9.x2) | copy-start | bytes 442372
  38.2 1.8 %collective-permute-start.11 = (bf16[2,72,1024]{2,1,0:T(8,128)(2,1)S(1)}, bf16[2,72,1024]{2,1,0:T(8,128)(2,1)S(1)}, u32[]{:S(2)}, u32[]{:S(2)}) collective-permute-start(bf16[2,72,1024]{2,1,0:T(8,128)(2,1)S(1)} %pad_maximum_fusion.3), channel_id=1, source_target_pairs={{0,1},{1,0},{2,3},{3,2},{4,5},{5,4},{6,7},{7,6},{8,9},{9,8},{10,11... | collective-permute-start | bytes 884744 | tf_op jit(solution)/shard_map/ppermute | solution.py:225
  40.1 5.3 %copy-start.9 = (bf16[2,72,1024]{2,1,0:T(8,128)(2,1)}, bf16[2,72,1024]{2,1,0:T(8,128)(2,1)S(1)}, u32[]{:S(2)}) copy-start(bf16[2,72,1024]{2,1,0:T(8,128)(2,1)S(1)} %collective-permute-done.11.c2) | copy-start | bytes 884740
  49.7 8.8 %copy-start.5 = (bf16[2,128,1024]{2,1,0:T(8,128)(2,1)}, bf16[2,128,1024]{2,1,0:T(8,128)(2,1)S(1)}, u32[]{:S(2)}) copy-start(bf16[2,128,1024]{2,1,0:T(8,128)(2,1)S(1)} %collective-permute-done.3.t1) | copy-start | bytes 1572868
  55.2 3.2 %copy-start.6 = (bf16[2,128,1024]{2,1,0:T(8,128)(2,1)}, bf16[2,128,1024]{2,1,0:T(8,128)(2,1)S(1)}, u32[]{:S(2)}) copy-start(bf16[2,128,1024]{2,1,0:T(8,128)(2,1)S(1)} %collective-permute-done.8.t2) | copy-start | bytes 1572868
